TPU v7x, 32 devices: a whole 2x2x4 slice. The times are simulated.
32 devices in a mesh: dp: 4 (over z), mp: 8 (over y, x, core).
Axes of the slice: x: 2, y: 2, z: 4, core: 2. Of those that a mesh axis runs over, the one named last changes fastest.
Arguments:
- block_input: bfloat16 [8192, 2048], P(('dp', 'mp')), may hold values from -6 to 6
- out_cotangent: bfloat16 [8192, 2048], P(('dp', 'mp')), may hold values from -6 to 6
- objective: int32 [16], P('dp'), may hold values from 0 to 1, as said below
- prefix_len: int32 [16], P('dp'), may hold values from 64 to 511
- target_mask: int32 [8192], P(('dp', 'mp')), may hold values from 0 to 1, as said below
- qkv_weight: float32 [2048, 3, 2048], P('dp', None, 'mp'), may hold values from -0.125 to 0.125
- out_weight: float32 [2048, 2048], P('mp', 'dp'), may hold values from -3 to 3
- gateup_weight: float32 [2048, 2, 5472], P('dp', None, 'mp'), may hold values from -0.125 to 0.125
- down_weight: float32 [5472, 2048], P('mp', 'dp'), may hold values from -0.625 to 0.625
- norm_params: float32 [4, 2048], replicated, as said below
- qkv_first: float32 [2048, 3, 2048], P('dp', None, 'mp'), may hold values from -0.125 to 0.125
- out_first: float32 [2048, 2048], P('mp', 'dp'), may hold values from -0.005859375 to 0.005859375
- gateup_first: float32 [2048, 2, 5472], P('dp', None, 'mp'), may hold values from -0.09375 to 0.09375
- down_first: float32 [5472, 2048], P('mp', 'dp'), may hold values from -0.013671875 to 0.013671875
- norm_first: float32 [4, 2048], replicated, may hold values from -0.21875 to 0.21875
- qkv_second: float32 [2048, 3, 2048], P('dp', None, 'mp'), may hold values from 3.0517578e-05 to 0.00048828125
- out_second: float32 [2048, 2048], P('mp', 'dp'), may hold values from 7.080078e-08 to 1.1230469e-06
- gateup_second: float32 [2048, 2, 5472], P('dp', None, 'mp'), may hold values from 1.953125e-05 to 0.0003125
- down_second: float32 [5472, 2048], P('mp', 'dp'), may hold values from 4.3945312e-07 to 7.080078e-06
- norm_second: float32 [4, 2048], replicated, may hold values from 0.00012207031 to 0.001953125
Outputs:
- block_output: bfloat16 [8192, 2048], P(('dp', 'mp'))
- input_grad: float32 [8192, 2048], P(('dp', 'mp'))
- qkv_new: float32 [2048, 3, 2048], P('dp', None, 'mp')
- qkv_first_new: float32 [2048, 3, 2048], P('dp', None, 'mp')
- qkv_second_new: float32 [2048, 3, 2048], P('dp', None, 'mp')
- out_new: float32 [2048, 2048], P('mp', 'dp')
- out_first_new: float32 [2048, 2048], P('mp', 'dp')
- out_second_new: float32 [2048, 2048], P('mp', 'dp')
- gateup_new: float32 [2048, 2, 5472], P('dp', None, 'mp')
- gateup_first_new: float32 [2048, 2, 5472], P('dp', None, 'mp')
- gateup_second_new: float32 [2048, 2, 5472], P('dp', None, 'mp')
- down_new: float32 [5472, 2048], P('mp', 'dp')
- down_first_new: float32 [5472, 2048], P('mp', 'dp')
- down_second_new: float32 [5472, 2048], P('mp', 'dp')
- norm_new: float32 [4, 2048], replicated
- norm_first_new: float32 [4, 2048], replicated
- norm_second_new: float32 [4, 2048], replicated
Inputs may be any that keep to these rules, and one draw needn't show every extreme that they name: `objective`: at least one sequence of each kind. `target_mask`: the last residue of every sequence is a target. `norm_params`: rows 0 and 2 are the gains of the first and second norm, rows 1 and 3 their biases.
All inputs are finite; a program needn't handle non-finite values.
Results may differ from a plain program's by a relative error of at most 0.024.
Values may be sent and summed in bfloat16 or wider, within the bound.
No kernel may reach another device: no remote copies, remote signals or barrier semaphores. Data moves between devices by JAX's collectives and lax.ppermute only.
A program may use at most 256 MiB of HBM per device.

v0:
```python
import jax
import jax.numpy as jnp
from jax import lax
from jax.sharding import PartitionSpec as P

D = 2048
HD = 128
FF = 5461
FF_PAD = 5472
STEP = 5
deep_alpha = 48.0**0.5
norm_eps = 1e-05
masked_score = -1e30
rope_base = 10000.0
beta_one = 0.5
beta_two = 0.5
adam_eps = 1e-08
decay_rate = 0.1


def rope_tables(seq_len, head_dim):
    position = jnp.arange(seq_len, dtype=jnp.float32)
    freqs = rope_base ** (-jnp.arange(0, head_dim, 2, dtype=jnp.float32) / head_dim)
    angles = position[:, None] * freqs[None, :]
    return (jnp.cos(angles), jnp.sin(angles))


def rotate(values, cosine, sine_table):
    half_dim = values.shape[-1] // 2
    first_half = values[..., :half_dim]
    second_half = values[..., half_dim:]
    cos_b = cosine[:, None, :]
    sin_b = sine_table[:, None, :]
    return jnp.concatenate(
        [first_half * cos_b - second_half * sin_b, second_half * cos_b + first_half * sin_b], -1
    )


def norm_forward(hidden, norm_gain, norm_bias):
    row_mean = jnp.mean(hidden, -1, keepdims=True)
    centred = hidden - row_mean
    variance = jnp.mean(centred * centred, -1, keepdims=True)
    inv_std = lax.rsqrt(variance + norm_eps)
    normed = centred * inv_std
    return (normed * norm_gain + norm_bias, normed, inv_std)


def norm_backward(grad_rows, normed, inv_std, norm_gain):
    grad_normed = grad_rows * norm_gain
    mean_grad = jnp.mean(grad_normed, -1, keepdims=True)
    mean_proj = jnp.mean(grad_normed * normed, -1, keepdims=True)
    grad_in = inv_std * (grad_normed - mean_grad - normed * mean_proj)
    return (grad_in, jnp.sum(grad_rows * normed, 0), jnp.sum(grad_rows, 0))


def adamw(weight, gradient, first_moment, second, step_rate):
    first_new = beta_one * first_moment + (1.0 - beta_one) * gradient
    second_new = beta_two * second + (1.0 - beta_two) * gradient * gradient
    first_hat = first_new / (1.0 - beta_one**STEP)
    second_hat = second_new / (1.0 - beta_two**STEP)
    weight_new = weight - step_rate * (
        first_hat / (jnp.sqrt(second_hat) + adam_eps) + decay_rate * weight
    )
    return (weight_new, first_new, second_new)


def local(
    block_input,
    out_cotangent,
    objective,
    prefix_len,
    target_mask,
    qkv_weight,
    out_weight,
    gateup_weight,
    down_weight,
    norm_params,
    qkv_first,
    out_first,
    gateup_first,
    down_first,
    norm_first,
    qkv_second,
    out_second,
    gateup_second,
    down_second,
    norm_second,
):
    mp_count = lax.axis_size("mp")
    mp_index = lax.axis_index("mp")
    own_rows = block_input.shape[0]
    seq_count = objective.shape[0]
    group_rows = own_rows * mp_count
    seq_len = group_rows // seq_count
    local_dim = qkv_weight.shape[2]
    local_heads = local_dim // HD
    local_units = gateup_weight.shape[2]
    score_scale = HD ** (-0.5)
    row_start = mp_index * own_rows
    qkv_full, out_full, gateup_full, down_full = (
        lax.all_gather(qkv_weight.astype(jnp.bfloat16), "dp", axis=0, tiled=True),
        lax.all_gather(out_weight.astype(jnp.bfloat16), "dp", axis=1, tiled=True),
        lax.all_gather(gateup_weight.astype(jnp.bfloat16), "dp", axis=0, tiled=True),
        lax.all_gather(down_weight.astype(jnp.bfloat16), "dp", axis=1, tiled=True),
    )
    input_all = lax.all_gather(block_input, "mp", axis=0, tiled=True)
    projected = jnp.einsum("td,dce->tce", input_all, qkv_full, preferred_element_type=jnp.float32)
    shaped = projected.reshape(seq_count, seq_len, 3, local_heads, HD)
    cosine, sine_table = rope_tables(seq_len, HD)
    query_rows = rotate(shaped[:, :, 0], cosine, sine_table).astype(jnp.bfloat16)
    key_rows = rotate(shaped[:, :, 1], cosine, sine_table).astype(jnp.bfloat16)
    value_rows = shaped[:, :, 2].astype(jnp.bfloat16)
    row_index = jnp.arange(seq_len)[:, None]
    col_index = jnp.arange(seq_len)[None, :]
    visible = (
        (objective[:, None, None] > 0)
        | (col_index[None] < prefix_len[:, None, None])
        | (col_index <= row_index)[None]
    )
    scores = (
        jnp.einsum("sihe,sjhe->shij", query_rows, key_rows, preferred_element_type=jnp.float32)
        * score_scale
    )
    scores = jnp.where(visible[:, None], scores, masked_score)
    row_max = jnp.max(scores, -1, keepdims=True)
    exp_scores = jnp.exp(scores - row_max)
    row_total = jnp.sum(exp_scores, -1, keepdims=True)
    soft_weights = exp_scores / row_total
    log_total = row_max + jnp.log(row_total)
    attended = jnp.einsum(
        "shij,sjhe->sihe",
        soft_weights.astype(jnp.bfloat16),
        value_rows,
        preferred_element_type=jnp.float32,
    )
    attended_low = attended.reshape(group_rows, local_dim).astype(jnp.bfloat16)
    attn_part = jnp.dot(attended_low, out_full, preferred_element_type=jnp.float32)
    attn_total = lax.psum(attn_part, "mp")
    hidden_all = deep_alpha * input_all.astype(jnp.float32) + attn_total
    middle_all, _, _ = norm_forward(hidden_all, norm_params[0], norm_params[1])
    middle_low = middle_all.astype(jnp.bfloat16)
    hidden_one = lax.dynamic_slice_in_dim(hidden_all, row_start, own_rows, 0)
    middle = lax.dynamic_slice_in_dim(middle_all, row_start, own_rows, 0)
    live_units = (mp_index * local_units + jnp.arange(local_units) < FF).astype(jnp.float32)
    gate_up = jnp.einsum("td,dcf->tcf", middle_low, gateup_full, preferred_element_type=jnp.float32)
    hidden_low = (jax.nn.gelu(gate_up[:, 0]) * gate_up[:, 1] * live_units).astype(jnp.bfloat16)
    ffn_part = jnp.dot(hidden_low, down_full, preferred_element_type=jnp.float32)
    ffn_total = lax.psum(ffn_part.astype(jnp.bfloat16), "mp").astype(jnp.float32)
    ffn_own = lax.dynamic_slice_in_dim(ffn_total, row_start, own_rows, 0)
    hidden_two = deep_alpha * middle + ffn_own
    output_rows, normed_two, inv_two = norm_forward(hidden_two, norm_params[2], norm_params[3])
    mask_f32 = target_mask.astype(jnp.float32)
    grad_rows = out_cotangent.astype(jnp.float32) * mask_f32[:, None]
    grad_two, gain_two, bias_two = norm_backward(grad_rows, normed_two, inv_two, norm_params[2])
    ffn_back = lax.all_gather(grad_two.astype(jnp.bfloat16), "mp", axis=0, tiled=True)
    gate_again = jnp.einsum(
        "td,dcf->tcf", middle_low, gateup_full, preferred_element_type=jnp.float32
    )
    gate_act, gelu_pull = jax.vjp(jax.nn.gelu, gate_again[:, 0])
    up_part = gate_again[:, 1]
    hidden_again = (gate_act * up_part * live_units).astype(jnp.bfloat16)
    grad_hidden = (
        jnp.einsum("td,fd->tf", ffn_back, down_full, preferred_element_type=jnp.float32)
        * live_units
    )
    down_grad = jnp.einsum("tf,td->fd", hidden_again, ffn_back, preferred_element_type=jnp.float32)
    grad_gate = gelu_pull(grad_hidden * up_part)[0]
    grad_up = grad_hidden * gate_act
    grad_gateup = jnp.stack([grad_gate, grad_up], 1).astype(jnp.bfloat16)
    middle_part = jnp.einsum(
        "tcf,dcf->td", grad_gateup, gateup_full, preferred_element_type=jnp.float32
    )
    gateup_grad = jnp.einsum(
        "td,tcf->dcf", middle_low, grad_gateup, preferred_element_type=jnp.float32
    )
    grad_middle = (
        lax.psum_scatter(
            middle_part.astype(jnp.bfloat16), "mp", scatter_dimension=0, tiled=True
        ).astype(jnp.float32)
        + deep_alpha * grad_two
    )
    _, normed_one, inv_one = norm_forward(hidden_one, norm_params[0], norm_params[1])
    grad_one, gain_one, bias_one = norm_backward(grad_middle, normed_one, inv_one, norm_params[0])
    attn_back = lax.all_gather(grad_one.astype(jnp.bfloat16), "mp", axis=0, tiled=True)
    grad_attended = jnp.einsum(
        "td,ed->te", attn_back, out_full, preferred_element_type=jnp.float32
    ).astype(jnp.bfloat16)
    grad_attended = grad_attended.reshape(seq_count, seq_len, local_heads, HD)
    out_grad = jnp.einsum("te,td->ed", attended_low, attn_back, preferred_element_type=jnp.float32)
    scores_again = (
        jnp.einsum("sihe,sjhe->shij", query_rows, key_rows, preferred_element_type=jnp.float32)
        * score_scale
    )
    scores_again = jnp.where(visible[:, None], scores_again, masked_score)
    soft_again = jnp.exp(scores_again - log_total)
    grad_soft = jnp.einsum(
        "sihe,sjhe->shij", grad_attended, value_rows, preferred_element_type=jnp.float32
    )
    value_grad = jnp.einsum(
        "shij,sihe->sjhe",
        soft_again.astype(jnp.bfloat16),
        grad_attended,
        preferred_element_type=jnp.float32,
    )
    row_dot = jnp.sum(soft_again * grad_soft, -1, keepdims=True)
    grad_scores = (soft_again * (grad_soft - row_dot)).astype(jnp.bfloat16)
    query_grad = (
        jnp.einsum("shij,sjhe->sihe", grad_scores, key_rows, preferred_element_type=jnp.float32)
        * score_scale
    )
    key_grad = (
        jnp.einsum("shij,sihe->sjhe", grad_scores, query_rows, preferred_element_type=jnp.float32)
        * score_scale
    )
    query_lin = rotate(query_grad, cosine, -sine_table)
    key_lin = rotate(key_grad, cosine, -sine_table)
    grad_proj = (
        jnp.stack([query_lin, key_lin, value_grad], 2)
        .astype(jnp.bfloat16)
        .reshape(group_rows, 3, local_dim)
    )
    input_part = jnp.einsum("tce,dce->td", grad_proj, qkv_full, preferred_element_type=jnp.float32)
    qkv_grad = jnp.einsum("td,tce->dce", input_all, grad_proj, preferred_element_type=jnp.float32)
    input_raw = (
        lax.psum_scatter(
            input_part.astype(jnp.bfloat16), "mp", scatter_dimension=0, tiled=True
        ).astype(jnp.float32)
        + deep_alpha * grad_one
    )
    qkv_grad, out_grad, gateup_grad, down_grad = (
        lax.psum_scatter(
            qkv_grad.astype(jnp.bfloat16), "dp", scatter_dimension=0, tiled=True
        ).astype(jnp.float32),
        lax.psum_scatter(
            out_grad.astype(jnp.bfloat16), "dp", scatter_dimension=1, tiled=True
        ).astype(jnp.float32),
        lax.psum_scatter(
            gateup_grad.astype(jnp.bfloat16), "dp", scatter_dimension=0, tiled=True
        ).astype(jnp.float32),
        lax.psum_scatter(
            down_grad.astype(jnp.bfloat16), "dp", scatter_dimension=1, tiled=True
        ).astype(jnp.float32),
    )
    norm_grad = jnp.stack([gain_one, bias_one, gain_two, bias_two], 0)
    norm_grad, target_count = lax.psum((norm_grad, jnp.sum(mask_f32)), ("dp", "mp"))
    rate_list = (D ** (-0.5), 0.5, D ** (-0.5), (FF_PAD // 64) ** (-0.5), 0.4)
    qkv_res = adamw(qkv_weight, qkv_grad / target_count, qkv_first, qkv_second, rate_list[0])
    out_res = adamw(out_weight, out_grad / target_count, out_first, out_second, rate_list[1])
    gateup_res = adamw(
        gateup_weight, gateup_grad / target_count, gateup_first, gateup_second, rate_list[2]
    )
    down_res = adamw(down_weight, down_grad / target_count, down_first, down_second, rate_list[3])
    norm_res = adamw(norm_params, norm_grad / target_count, norm_first, norm_second, rate_list[4])
    return (
        output_rows.astype(jnp.bfloat16),
        input_raw / target_count,
        qkv_res[0],
        qkv_res[1],
        qkv_res[2],
        out_res[0],
        out_res[1],
        out_res[2],
        gateup_res[0],
        gateup_res[1],
        gateup_res[2],
        down_res[0],
        down_res[1],
        down_res[2],
        norm_res[0],
        norm_res[1],
        norm_res[2],
    )


def solution(mesh):
    return jax.shard_map(
        local,
        mesh=mesh,
        in_specs=(
            P(("dp", "mp"), None),
            P(("dp", "mp"), None),
            P("dp"),
            P("dp"),
            P(("dp", "mp")),
            P("dp", None, "mp"),
            P("mp", "dp"),
            P("dp", None, "mp"),
            P("mp", "dp"),
            P(),
            P("dp", None, "mp"),
            P("mp", "dp"),
            P("dp", None, "mp"),
            P("mp", "dp"),
            P(),
            P("dp", None, "mp"),
            P("mp", "dp"),
            P("dp", None, "mp"),
            P("mp", "dp"),
            P(),
        ),
        out_specs=(
            P(("dp", "mp"), None),
            P(("dp", "mp"), None),
            P("dp", None, "mp"),
            P("dp", None, "mp"),
            P("dp", None, "mp"),
            P("mp", "dp"),
            P("mp", "dp"),
            P("mp", "dp"),
            P("dp", None, "mp"),
            P("dp", None, "mp"),
            P("dp", None, "mp"),
            P("mp", "dp"),
            P("mp", "dp"),
            P("mp", "dp"),
            P(),
            P(),
            P(),
        ),
        check_vma=False,
    )
```

profile of v0, /device:TPU:0, one launch (start us, length us, event | category | flops | bytes accessed | tf_op | source)
XLA Modules:
  0.0 1279.1 jit_solution(2433256142239264889)
XLA Ops:
  14.7 61.7 %all-gather.10.cloned.1.call-done = bf16[2048,3,256]{2,0,1:T(8,128)(2,1)} async-done(((bf16[512,3,256]{2,0,1:T(8,128)(2,1)}), bf16[2048,3,256]{2,0,1:T(8,128)(2,1)}) %all-gather.10.cloned.1.call-update) | async-done | bytes 3145744 | tf_op jit(solution)/shard_map/all_gather | solution.py:101
  76.4 54.8 %all-gather.8.cloned.1.call-done = bf16[2048,2048]{1,0:T(8,128)(2,1)} async-done(((bf16[256,2048]{1,0:T(8,128)(2,1)}), bf16[2048,2048]{1,0:T(8,128)(2,1)}) %all-gather.8.cloned.1.call-update) | async-done | bytes 8388624 | tf_op jit(solution)/shard_map/all_gather | solution.py:106
  131.2 11.6 fusion.6
  142.8 8.3 reshape.239
  151.1 3.9 fusion.82
  155.0 3.3 slice.73
  173.4 11.4 copy.105
  184.8 9.7 fusion.51
  200.8 211.6 %all-reduce.4.cloned.1.call-done = f32[2048,2048]{1,0:T(8,128)} async-done(((f32[2048,2048]{1,0:T(8,128)}), f32[2048,2048]{1,0:T(8,128)}) %all-reduce.4.cloned.1.call-update) | async-done | bytes 16777232 | tf_op jit(solution)/shard_map/psum | solution.py:138
  412.5 16.0 %fusion.81 = (f32[2048]{0:T(1024)S(1)}, f32[2048,2048]{1,0:T(8,128)}) fusion(f32[2048,2048]{1,0:T(8,128)} %all-reduce.4.cloned.1.call-done, bf16[2048,2048]{1,0:T(8,128)(2,1)} %all-gather.8.cloned.1.call-done), kind=kLoop, calls=%fused_computation.166 | loop fusion | flops 16775168 | bytes 41951232 | tf_op jit(solution)/shard_map/reduce_sum | solution.py:40
  428.5 7.7 multiply_reduce_fusion
  436.2 12.2 multiply_add_fusion
  448.5 69.6 %all-gather.14.cloned.1.call-done = bf16[2048,2,684]{0,1,2:T(2,128)(2,1)} async-done(((bf16[512,2,684]{0,1,2:T(2,128)(2,1)}), bf16[2048,2,684]{0,1,2:T(2,128)(2,1)}) %all-gather.14.cloned.1.call-update) | async-done | bytes 5603344 | tf_op jit(solution)/shard_map/all_gather | solution.py:103
  518.1 22.3 %fusion.2 = f32[2048,2,684]{0,2,1:T(8,128)} fusion(bf16[2048,2,684]{0,1,2:T(2,128)(2,1)} %all-gather.14.cloned.1.call-done, f32[2048,2048]{1,0:T(8,128)} %multiply_add_fusion), kind=kOutput, calls=%fused_computation.7 | convolution fusion | flops 11479810048 | bytes 33587200 | tf_op jit(solution)/shard_map/td,dcf->tcf/dot_general | solution.py:145
  540.3 5.5 multiply_convert_fusion.2
  545.8 30.5 %all-gather.16.cloned.1.call-done = bf16[684,2048]{1,0:T(8,128)(2,1)} async-done(((bf16[684,512]{1,0:T(8,128)(2,1)}), bf16[684,2048]{1,0:T(8,128)(2,1)}) %all-gather.16.cloned.1.call-update) | async-done | bytes 2801680 | tf_op jit(solution)/shard_map/all_gather | solution.py:104
  576.3 11.2 convolution_convert_fusion
  588.2 124.4 %all-reduce.6.cloned.1.call-done = bf16[2048,2048]{1,0:T(8,128)(2,1)} async-done(((bf16[2048,2048]{1,0:T(8,128)(2,1)}), bf16[2048,2048]{1,0:T(8,128)(2,1)}) %all-reduce.6.cloned.1.call-update) | async-done | bytes 8388624 | tf_op jit(solution)/shard_map/psum | solution.py:148
  719.2 54.5 %all-gather.18.cloned.1.call-done = bf16[2048,2048]{1,0:T(8,128)(2,1)} async-done(((bf16[256,2048]{1,0:T(8,128)(2,1)}), bf16[2048,2048]{1,0:T(8,128)(2,1)}) %all-gather.18.cloned.1.call-update) | async-done | bytes 8388624 | tf_op jit(solution)/shard_map/all_gather | solution.py:155
  773.7 15.4 %fusion.36 = (bf16[2048,1,684]{0,2,1:T(8,128)(2,1)S(1)}, bf16[2048,1,684]{0,2,1:T(8,128)(2,1)S(1)}) fusion(f32[2048,2,684]{0,2,1:T(8,128)} %fusion.2, f32[684]{0:T(1024)S(1)} %fusion.66, bf16[2048,2048]{1,0:T(8,128)(2,1)} %all-gather.18.cloned.1.call-done, bf16[684,2048]{1,0:T(8,128)(2,1)} %all-gather.16.cloned.1.call-done), kind=kOutput, calls=%fused_computation.56 | convolution fusion | flops 5772828672 | bytes 28002992 | tf_op jit(solution)/shard_map/td,fd->tf/dot_general | solution.py:163
  791.6 17.9 %bitcast_convert_fusion.1 = bf16[2048,2048]{1,0:T(8,128)(2,1)} fusion(bf16[2048,2,684]{0,1,2:T(2,128)(2,1)} %all-gather.14.cloned.1.call-done, bf16[2048,1,684]{0,2,1:T(8,128)(2,1)S(1)} %get-tuple-element.102, bf16[2048,1,684]{0,2,1:T(8,128)(2,1)S(1)} %get-tuple-element.101), kind=kOutput, calls=%fused_computation.1 | convolution fusion | flops 11482611712 | bytes 19595264 | tf_op jit(solution)/shard_map/tcf,dcf->td/dot_general | solution.py:170
  813.5 67.7 %reduce-scatter.7.cloned.1.call-done = bf16[256,2048]{1,0:T(8,128)(2,1)} async-done(((bf16[2048,2048]{1,0:T(8,128)(2,1)}), bf16[256,2048]{1,0:T(8,128)(2,1)}) %reduce-scatter.7.cloned.1.call-update) | async-done | bytes 1048592 | tf_op jit(solution)/shard_map/reduce_scatter | solution.py:177
  884.2 4.1 fusion.78
  888.4 18.6 %fusion.19 = bf16[2048,2,684]{0,2,1:T(8,128)(2,1)} fusion(f32[2048,2048]{1,0:T(8,128)} %multiply_add_fusion, bf16[2048,1,684]{0,2,1:T(8,128)(2,1)} %copy-done.49, bf16[2048,1,684]{0,2,1:T(8,128)(2,1)} %copy-done.48), kind=kOutput, calls=%fused_computation.39 | convolution fusion | flops 11493818368 | bytes 27983872 | tf_op jit(solution)/shard_map/td,tcf->dcf/dot_general | solution.py:173
  908.8 10.6 convolution_convert_fusion.1
  920.2 22.6 %all-gather.20.cloned.1.call-done = bf16[2048,2048]{1,0:T(8,128)(2,1)} async-done(((bf16[256,2048]{1,0:T(8,128)(2,1)}), bf16[2048,2048]{1,0:T(8,128)(2,1)}) %all-gather.20.cloned.1.call-update) | async-done | bytes 8388624 | tf_op jit(solution)/shard_map/all_gather | solution.py:184
  942.7 5.8 convolution_convert_fusion.3
  949.6 6.0 fusion.46
  959.4 4.5 multiply_reduce_fusion.1
  964.0 4.8 multiply_convert_fusion
  984.3 6.8 convolution_convert_fusion.2
  993.3 12.0 fusion.31
  1007.1 10.8 bitcast_convert_fusion
  1027.8 41.6 %all-reduce = (f32[]{:T(128)}, f32[4,2048]{1,0:T(4,128)S(1)}) all-reduce(f32[]{:T(128)} %convert_reduce_fusion, f32[4,2048]{1,0:T(4,128)S(1)} %pad_maximum_fusion.11), channel_id=1, replica_groups=mesh['dp'=4,'mp'=8] {'dp','mp'}, use_global_device_ids=true, to_apply=%region_18.19 | all-reduce | flops 8193 | bytes 65544 | tf_op jit(solution)/shard_map/psum | solution.py:245
  1069.5 5.2 multiply_subtract_fusion
  1074.7 3.7 copy.133
  1078.4 3.7 copy.134
  1082.2 3.7 copy.135
  1087.2 16.2 %reduce-scatter.17.cloned.1.call-done = bf16[684,512]{1,0:T(8,128)(2,1)} async-done(((bf16[684,2048]{1,0:T(8,128)(2,1)}), bf16[684,512]{1,0:T(8,128)(2,1)}) %reduce-scatter.17.cloned.1.call-update) | async-done | bytes 700432 | tf_op jit(solution)/shard_map/reduce_scatter | solution.py:240
  1103.5 5.1 multiply_subtract_fusion.2
  1108.6 24.2 %reduce-scatter.13.cloned.1.call-done = bf16[256,512]{1,0:T(8,128)(2,1)} async-done(((bf16[256,2048]{1,0:T(8,128)(2,1)}), bf16[256,512]{1,0:T(8,128)(2,1)}) %reduce-scatter.13.cloned.1.call-update) | async-done | bytes 262160 | tf_op jit(solution)/shard_map/reduce_scatter | solution.py:234
  1132.8 3.6 multiply_subtract_fusion.3
  1136.4 57.5 %reduce-scatter.11.cloned.1.call-done = bf16[512,3,256]{0,2,1:T(8,128)(2,1)} async-done(((bf16[2048,3,256]{0,2,1:T(8,128)(2,1)}), bf16[512,3,256]{0,2,1:T(8,128)(2,1)}) %reduce-scatter.11.cloned.1.call-update) | async-done | bytes 786448 | tf_op jit(solution)/shard_map/reduce_scatter | solution.py:231
  1193.9 5.5 multiply_subtract_fusion.1
  1202.4 3.2 copy.131
  1205.6 3.3 copy.132
  1208.9 59.7 %reduce-scatter.9.cloned.1.call-done = bf16[256,2048]{1,0:T(8,128)(2,1)} async-done(((bf16[2048,2048]{1,0:T(8,128)(2,1)}), bf16[256,2048]{1,0:T(8,128)(2,1)}) %reduce-scatter.9.cloned.1.call-update) | async-done | bytes 1048592 | tf_op jit(solution)/shard_map/reduce_scatter | solution.py:225
  1268.6 3.5 add_divide_fusion
  (192 shorter events, 86.6 us)
Async XLA Ops:
  7.2 3.3 copy-start.28
  7.2 6.0 copy-start.47
  7.2 6.0 copy-start.46
  7.2 69.1 %all-gather.10.cloned.1.call-start = ((), (), s32[]{:S(2)}) async-start(), calls=%async_computation.7 | async-start | bytes 3932160 | tf_op jit(solution)/shard_map/all_gather | solution.py:101
  9.7 121.5 %all-gather.8.cloned.1.call-start = ((), (), s32[]{:S(2)}) async-start(), calls=%async_computation.6 | async-start | bytes 9437184 | tf_op jit(solution)/shard_map/all_gather | solution.py:106
  10.5 174.4 %all-gather.12.cloned.1.call-start = ((), (), s32[]{:S(2)}) async-start(), calls=%async_computation.8 | async-start | bytes 1310720 | tf_op jit(solution)/shard_map/all_gather | solution.py:102
  11.3 401.2 %all-reduce.4.cloned.1.call-start = ((), (), s32[]{:S(2)}) async-start(), calls=%async_computation.9 | async-start | bytes 33554432 | tf_op jit(solution)/shard_map/psum | solution.py:138
  13.2 150.0 %copy-start.26 = (f32[512,64]{1,0:T(8,128)}, f32[512,64]{1,0:T(8,128)S(1)}, u32[]{:S(2)}) copy-start(f32[512,64]{1,0:T(8,128)S(1)} %get-tuple-element.124) | copy-start | bytes 393220
  160.7 8.2 copy-start.14
  164.7 3.0 copy-start.5
  164.7 3.0 copy-start.7
  164.7 3.0 copy-start.9
  164.7 3.0 copy-start.11
  167.7 3.3 copy-start
  167.7 3.4 copy-start.34
  184.8 9.7 copy-start.1
  194.5 323.5 %all-gather.14.cloned.1.call-start = ((), (), s32[]{:S(2)}) async-start(), calls=%async_computation.10 | async-start | bytes 7004160 | tf_op jit(solution)/shard_map/all_gather | solution.py:103
  198.4 377.9 %all-gather.16.cloned.1.call-start = ((), (), s32[]{:S(2)}) async-start(), calls=%async_computation.11 | async-start | bytes 3522560 | tf_op jit(solution)/shard_map/all_gather | solution.py:104
  200.7 511.8 %all-reduce.6.cloned.1.call-start = ((), (), s32[]{:S(2)}) async-start(), calls=%async_computation.12 | async-start | bytes 16777216 | tf_op jit(solution)/shard_map/psum | solution.py:148
  545.8 41.6 %copy-start.24 = (bf16[2048,684]{0,1:T(8,128)(2,1)}, bf16[2048,684]{0,1:T(8,128)(2,1)S(1)}, u32[]{:S(2)}) copy-start(bf16[2048,684]{0,1:T(8,128)(2,1)S(1)} %multiply_convert_fusion.2) | copy-start | bytes 8404996
  587.5 186.2 %all-gather.18.cloned.1.call-start = ((), (), s32[]{:S(2)}) async-start(), calls=%async_computation.13 | async-start | bytes 9437184 | tf_op jit(solution)/shard_map/all_gather | solution.py:155
  588.2 127.0 %copy-start.20 = (bf16[256,2048]{1,0:T(8,128)(2,1)S(1)}, bf16[256,2048]{1,0:T(8,128)(2,1)}, u32[]{:S(2)}) copy-start(bf16[256,2048]{1,0:T(8,128)(2,1)} %param.21) | copy-start | bytes 3145732
  719.1 162.0 %reduce-scatter.7.cloned.1.call-start = ((), (), s32[]{:S(2)}) async-start(), calls=%async_computation.14 | async-start | bytes 9437184 | tf_op jit(solution)/shard_map/reduce_scatter | solution.py:177
  809.5 133.2 %all-gather.20.cloned.1.call-start = ((), (), s32[]{:S(2)}) async-start(), calls=%async_computation.15 | async-start | bytes 9437184 | tf_op jit(solution)/shard_map/all_gather | solution.py:184
  881.2 3.0 copy-start.21
  888.3 181.1 %reduce-scatter.15.cloned.1.call-start = ((), (), s32[]{:S(2)}) async-start(), calls=%async_computation.19 | async-start | bytes 7045120 | tf_op jit(solution)/shard_map/reduce_scatter | solution.py:237
  907.0 196.4 %reduce-scatter.17.cloned.1.call-start = ((), (), s32[]{:S(2)}) async-start(), calls=%async_computation.20 | async-start | bytes 3522560 | tf_op jit(solution)/shard_map/reduce_scatter | solution.py:240
  919.4 23.3 %copy-start.30 = (bf16[256,2048]{1,0:T(8,128)(2,1)S(1)}, bf16[256,2048]{1,0:T(8,128)(2,1)}, u32[]{:S(2)}) copy-start(bf16[256,2048]{1,0:T(8,128)(2,1)} %all-gather.12.cloned.1.call-done) | copy-start | bytes 3145732
  919.5 213.3 %reduce-scatter.13.cloned.1.call-start = ((), (), s32[]{:S(2)}) async-start(), calls=%async_computation.18 | async-start | bytes 1310720 | tf_op jit(solution)/shard_map/reduce_scatter | solution.py:234
  955.6 3.8 copy-start.15
  963.9 4.8 copy-start.10
  963.9 4.8 copy-start.12
  979.4 4.9 copy-start.2
  984.3 6.9 copy-start.22
  991.1 202.7 %reduce-scatter.11.cloned.1.call-start = ((), (), s32[]{:S(2)}) async-start(), calls=%async_computation.17 | async-start | bytes 3932160 | tf_op jit(solution)/shard_map/reduce_scatter | solution.py:231
  1005.3 263.3 %reduce-scatter.9.cloned.1.call-start = ((), (), s32[]{:S(2)}) async-start(), calls=%async_computation.16 | async-start | bytes 9437184 | tf_op jit(solution)/shard_map/reduce_scatter | solution.py:225
  1019.4 4.8 copy-start.45
  1019.4 5.4 copy-start.40
  1019.4 5.4 copy-start.41
  1021.0 48.5 %copy-start.4 = (f32[512,2,684]{0,1,2:T(2,128)S(1)}, f32[512,2,684]{0,1,2:T(2,128)}, u32[]{:S(2)}) copy-start(f32[512,2,684]{0,1,2:T(2,128)} %param.27) | copy-start | bytes 8404996
  1082.1 3.7 copy-start.37
  1082.1 3.7 copy-start.42
  1082.1 3.7 copy-start.43
  1082.1 21.3 %copy-start.19 = (f32[684,512]{1,0:T(8,128)S(1)}, f32[684,512]{1,0:T(8,128)}, u32[]{:S(2)}) copy-start(f32[684,512]{1,0:T(8,128)} %param.28) | copy-start | bytes 4202500
  1082.1 21.3 %copy-start.29 = (f32[684,512]{1,0:T(8,128)S(1)}, f32[684,512]{1,0:T(8,128)}, u32[]{:S(2)}) copy-start(f32[684,512]{1,0:T(8,128)} %param.33) | copy-start | bytes 4202500
  1108.6 85.3 %copy-start.17 = (f32[512,3,256]{0,2,1:T(8,128)S(1)}, f32[512,3,256]{0,2,1:T(8,128)}, u32[]{:S(2)}) copy-start(f32[512,3,256]{0,2,1:T(8,128)} %copy.125) | copy-start | bytes 4718596
  1108.6 85.3 %copy-start.18 = (f32[512,3,256]{0,2,1:T(8,128)S(1)}, f32[512,3,256]{0,2,1:T(8,128)}, u32[]{:S(2)}) copy-start(f32[512,3,256]{0,2,1:T(8,128)} %copy.121) | copy-start | bytes 4718596
  1202.4 66.2 %copy-start.13 = (f32[256,2048]{1,0:T(8,128)S(1)}, f32[256,2048]{1,0:T(8,128)}, u32[]{:S(2)}) copy-start(f32[256,2048]{1,0:T(8,128)} %get-tuple-element.94) | copy-start | bytes 6291460
  (17 other events, 26.7 us)
Sparse Core Ops, SparseCore 0:
  10.2 66.1 all-gather.9
  78.3 52.8 all-gather.7
  133.3 27.9 all-gather.11
  194.6 217.7 all-reduce.3
  414.4 103.5 all-gather.13
  520.0 56.2 all-gather.15
  587.6 124.8 all-reduce.5
  719.3 54.3 all-gather.17
  809.6 71.4 reduce-scatter.6
  888.5 54.2 all-gather.19
  945.1 100.1 reduce-scatter.14
  1047.4 55.9 reduce-scatter.16
  1105.7 26.9 reduce-scatter.12
  1134.9 58.8 reduce-scatter.10
  1197.2 71.3 reduce-scatter.8
where the time goes:
time: 1290 us; the launch traced here: 1280 us
  waiting for transfers between devices  856 us (66%)
  matrix products  171 us (13%)
  other arithmetic  105 us (8%)
  local copies, waits for them, and re-layouts  89.7 us (7%)
  blocking collectives  41.6 us (3%)
  between operations  15 us (1%)
    psum x1, waiting for transfers between devices, local(): attn_total = lax.psum(attn_part, 'mp')  212 us
    psum x1, waiting for transfers between devices, local(): lax.psum(ffn_part.astype(jnp.bfloat16), 'mp').astype(jnp.float32)  124 us
    all_gather x1, waiting for transfers between devices, local(): lax.all_gather(gateup_weight.astype(jnp.bfloat16), 'dp', axis=0, tiled=True)  69.6 us
    reduce_scatter x1, waiting for transfers between devices, local(): lax.psum_scatter(middle_part.astype(jnp.bfloat16), 'mp', scatter_dimensio...  67.7 us
    all_gather x1, waiting for transfers between devices, local(): lax.all_gather(qkv_weight.astype(jnp.bfloat16), 'dp', axis=0, tiled=True)  61.7 us
    reduce_scatter x1, waiting for transfers between devices, local(): lax.psum_scatter(input_part.astype(jnp.bfloat16), 'mp', scatter_dimension...  59.7 us
    reduce_scatter x1, waiting for transfers between devices, local(): lax.psum_scatter(qkv_grad.astype(jnp.bfloat16), 'dp', scatter_dimension=0...  57.5 us
    all_gather x1, waiting for transfers between devices, local(): input_all = lax.all_gather(block_input, 'mp', axis=0, tiled=True)  54.8 us
  transfers between devices with their start and end apart: 15, of which 13 were waited for; matrix products, arithmetic and copies ran while one was open for 22% of the time, Pallas kernels for 0%

commit v1 on v0

--- a/solution.py
+++ b/solution.py
@@ -135,7 +135,11 @@
     )
     attended_low = attended.reshape(group_rows, local_dim).astype(jnp.bfloat16)
     attn_part = jnp.dot(attended_low, out_full, preferred_element_type=jnp.float32)
-    attn_total = lax.psum(attn_part, "mp")
+    attn_total = attn_part
+    for hop in (1, 2, 4):
+        attn_total = attn_total + lax.ppermute(
+            attn_total, "mp", [(dev, dev ^ hop) for dev in range(8)]
+        )
     hidden_all = deep_alpha * input_all.astype(jnp.float32) + attn_total
     middle_all, _, _ = norm_forward(hidden_all, norm_params[0], norm_params[1])
     middle_low = middle_all.astype(jnp.bfloat16)

time: 1290 us -> 1750 us (1.36)
  waiting for transfers between devices: 856 us -> 1280 us
  other arithmetic: 105 us -> 132 us
    ppermute x0 -> x3, waiting for transfers between devices: none -> 738 us  [local(): lax.ppermute(attn_total, 'mp', [(dev, dev ^ hop) for dev in range(8)])]
    psum x1 -> x0, waiting for transfers between devices: 212 us -> none  [local(): attn_total = lax.psum(attn_part, 'mp')]
    all_gather x1, waiting for transfers between devices: 69.6 us -> 0.01 us  [local(): lax.all_gather(gateup_weight.astype(jnp.bfloat16), 'dp', axis=0, tiled=True)]
    all_gather x1, waiting for transfers between devices: 30.5 us -> 0.02 us  [local(): lax.all_gather(down_weight.astype(jnp.bfloat16), 'dp', axis=1, tiled=True)]
    add x0 -> x2, other arithmetic: none -> 23.8 us  [local(): attn_total + lax.ppermute(attn_total, 'mp', [(dev, dev ^ hop) for dev in...]
    unnamed x112 -> x116, local copies, waits for them, and re-layouts: 47.2 us -> 50.9 us
  transfers between devices with their start and end apart: 15 -> 17, of which waited for: 13 -> 13; matrix products, arithmetic and copies ran while one was open for 22% -> 16% of each run, Pallas kernels for 0% -> 0%
where the time goes in v1:
time: 1750 us; the launch traced here: 1740 us
  waiting for transfers between devices  1280 us (73%)
  matrix products  166 us (9%)
  other arithmetic  132 us (8%)
  local copies, waits for them, and re-layouts  94.8 us (5%)
  blocking collectives  41.5 us (2%)
    ppermute x3, waiting for transfers between devices, local(): lax.ppermute(attn_total, 'mp', [(dev, dev ^ hop) for dev in range(8)])  738 us
    psum x1, waiting for transfers between devices, local(): lax.psum(ffn_part.astype(jnp.bfloat16), 'mp').astype(jnp.float32)  126 us
    reduce_scatter x1, waiting for transfers between devices, local(): lax.psum_scatter(middle_part.astype(jnp.bfloat16), 'mp', scatter_dimensio...  67.7 us
    all_gather x1, waiting for transfers between devices, local(): lax.all_gather(qkv_weight.astype(jnp.bfloat16), 'dp', axis=0, tiled=True)  61.7 us
    reduce_scatter x1, waiting for transfers between devices, local(): lax.psum_scatter(input_part.astype(jnp.bfloat16), 'mp', scatter_dimension...  59.7 us
    reduce_scatter x1, waiting for transfers between devices, local(): lax.psum_scatter(qkv_grad.astype(jnp.bfloat16), 'dp', scatter_dimension=0...  57.7 us
    all_gather x1, waiting for transfers between devices, local(): input_all = lax.all_gather(block_input, 'mp', axis=0, tiled=True)  54.8 us
    all_gather x1, waiting for transfers between devices, local(): lax.all_gather(grad_two.astype(jnp.bfloat16), 'mp', axis=0, tiled=True)  54.5 us
  transfers between devices with their start and end apart: 17, of which 13 were waited for; matrix products, arithmetic and copies ran while one was open for 16% of the time, Pallas kernels for 0%

profile of v1, /device:TPU:0, one launch (start us, length us, event | category | flops | bytes accessed | tf_op | source)
XLA Modules:
  0.0 1736.5 jit_solution(14238374968244462345)
XLA Ops:
  14.7 61.7 %all-gather.10.cloned.1.call-done = bf16[2048,3,256]{2,0,1:T(8,128)(2,1)} async-done(((bf16[512,3,256]{2,0,1:T(8,128)(2,1)}), bf16[2048,3,256]{2,0,1:T(8,128)(2,1)}) %all-gather.10.cloned.1.call-update) | async-done | bytes 3145744 | tf_op jit(solution)/shard_map/all_gather | solution.py:101
  76.4 54.8 %all-gather.8.cloned.1.call-done = bf16[2048,2048]{1,0:T(8,128)(2,1)} async-done(((bf16[256,2048]{1,0:T(8,128)(2,1)}), bf16[2048,2048]{1,0:T(8,128)(2,1)}) %all-gather.8.cloned.1.call-update) | async-done | bytes 8388624 | tf_op jit(solution)/shard_map/all_gather | solution.py:106
  131.2 11.6 fusion.6
  142.8 8.3 reshape.239
  151.1 3.9 fusion.82
  173.4 12.8 copy.109
  186.2 3.9 fusion.51
  190.5 5.4 copy-done.1
  195.9 19.6 %collective-permute-done = f32[2048,2048]{1,0:T(8,128)} collective-permute-done((f32[2048,2048]{1,0:T(8,128)S(1)}, f32[2048,2048]{1,0:T(8,128)}, u32[]{:S(2)}, u32[]{:S(2)}) %collective-permute-start) | collective-permute-done | bytes 16777248 | tf_op jit(solution)/shard_map/ppermute | solution.py:140
  215.5 11.6 add.207
  228.7 361.0 %collective-permute-done.1 = f32[2048,2048]{1,0:T(8,128)} collective-permute-done((f32[2048,2048]{1,0:T(8,128)S(1)}, f32[2048,2048]{1,0:T(8,128)}, u32[]{:S(2)}, u32[]{:S(2)}) %collective-permute-start.1) | collective-permute-done | bytes 16777248 | tf_op jit(solution)/shard_map/ppermute | solution.py:140
  589.8 12.1 add.208
  606.2 357.5 %collective-permute-done.2 = f32[2048,2048]{1,0:T(8,128)} collective-permute-done((f32[2048,2048]{1,0:T(8,128)}, f32[2048,2048]{1,0:T(8,128)}, u32[]{:S(2)}, u32[]{:S(2)}) %collective-permute-start.2) | collective-permute-done | bytes 16777248 | tf_op jit(solution)/shard_map/ppermute | solution.py:140
  963.7 20.6 %fusion.81 = (f32[2048]{0:T(1024)S(1)}, f32[2048,2048]{1,0:T(8,128)}) fusion(f32[2048,2048]{1,0:T(8,128)} %add.208, f32[2048,2048]{1,0:T(8,128)} %collective-permute-done.2, bf16[2048,2048]{1,0:T(8,128)(2,1)} %all-gather.8.cloned.1.call-done), kind=kLoop, calls=%fused_computation.166 | loop fusion | flops 20969472 | bytes 58728448 | tf_op jit(solution)/shard_map/reduce_sum | solution.py:40
  984.4 7.6 multiply_reduce_fusion
  992.0 12.2 multiply_add_fusion
  1004.2 22.3 %fusion.2 = f32[2048,2,684]{0,2,1:T(8,128)} fusion(bf16[2048,2,684]{0,1,2:T(2,128)(2,1)} %all-gather.14.cloned.1.call-done, f32[2048,2048]{1,0:T(8,128)} %multiply_add_fusion), kind=kOutput, calls=%fused_computation.7 | convolution fusion | flops 11479810048 | bytes 33587200 | tf_op jit(solution)/shard_map/td,dcf->tcf/dot_general | solution.py:149
  1026.5 5.5 multiply_convert_fusion.2
  1032.0 11.7 convolution_convert_fusion
  1044.4 125.7 %all-reduce.3.cloned.1.call-done = bf16[2048,2048]{1,0:T(8,128)(2,1)} async-done(((bf16[2048,2048]{1,0:T(8,128)(2,1)}), bf16[2048,2048]{1,0:T(8,128)(2,1)}) %all-reduce.3.cloned.1.call-update) | async-done | bytes 8388624 | tf_op jit(solution)/shard_map/psum | solution.py:152
  1176.7 54.5 %all-gather.18.cloned.1.call-done = bf16[2048,2048]{1,0:T(8,128)(2,1)} async-done(((bf16[256,2048]{1,0:T(8,128)(2,1)}), bf16[2048,2048]{1,0:T(8,128)(2,1)}) %all-gather.18.cloned.1.call-update) | async-done | bytes 8388624 | tf_op jit(solution)/shard_map/all_gather | solution.py:159
  1231.2 15.4 fusion.36
  1249.1 17.9 %bitcast_convert_fusion.1 = bf16[2048,2048]{1,0:T(8,128)(2,1)} fusion(bf16[2048,2,684]{0,1,2:T(2,128)(2,1)} %all-gather.14.cloned.1.call-done, bf16[2048,1,684]{0,2,1:T(8,128)(2,1)S(1)} %get-tuple-element.102, bf16[2048,1,684]{0,2,1:T(8,128)(2,1)S(1)} %get-tuple-element.101), kind=kOutput, calls=%fused_computation.1 | convolution fusion | flops 11482611712 | bytes 19595264 | tf_op jit(solution)/shard_map/tcf,dcf->td/dot_general | solution.py:174
  1271.0 67.7 %reduce-scatter.7.cloned.1.call-done = bf16[256,2048]{1,0:T(8,128)(2,1)} async-done(((bf16[2048,2048]{1,0:T(8,128)(2,1)}), bf16[256,2048]{1,0:T(8,128)(2,1)}) %reduce-scatter.7.cloned.1.call-update) | async-done | bytes 1048592 | tf_op jit(solution)/shard_map/reduce_scatter | solution.py:181
  1341.8 4.1 fusion.78
  1345.9 18.7 %fusion.19 = bf16[2048,2,684]{0,2,1:T(8,128)(2,1)} fusion(f32[2048,2048]{1,0:T(8,128)} %multiply_add_fusion, bf16[2048,1,684]{0,2,1:T(8,128)(2,1)} %copy-done.51, bf16[2048,1,684]{0,2,1:T(8,128)(2,1)} %copy-done.50), kind=kOutput, calls=%fused_computation.39 | convolution fusion | flops 11493818368 | bytes 27983872 | tf_op jit(solution)/shard_map/td,tcf->dcf/dot_general | solution.py:177
  1366.4 10.6 convolution_convert_fusion.1
  1377.8 22.5 %all-gather.20.cloned.1.call-done = bf16[2048,2048]{1,0:T(8,128)(2,1)} async-done(((bf16[256,2048]{1,0:T(8,128)(2,1)}), bf16[2048,2048]{1,0:T(8,128)(2,1)}) %all-gather.20.cloned.1.call-update) | async-done | bytes 8388624 | tf_op jit(solution)/shard_map/all_gather | solution.py:188
  1400.3 5.8 convolution_convert_fusion.3
  1407.2 6.0 fusion.46
  1417.0 4.6 multiply_reduce_fusion.1
  1421.6 4.8 multiply_convert_fusion
  1441.9 6.8 convolution_convert_fusion.2
  1450.9 12.0 fusion.31
  1464.8 10.8 bitcast_convert_fusion
  1485.5 41.5 %all-reduce = (f32[]{:T(128)}, f32[4,2048]{1,0:T(4,128)S(1)}) all-reduce(f32[]{:T(128)} %convert_reduce_fusion, f32[4,2048]{1,0:T(4,128)S(1)} %pad_maximum_fusion.11), channel_id=1, replica_groups=mesh['dp'=4,'mp'=8] {'dp','mp'}, use_global_device_ids=true, to_apply=%region_17.18 | all-reduce | flops 8193 | bytes 65544 | tf_op jit(solution)/shard_map/psum | solution.py:249
  1526.9 5.2 multiply_subtract_fusion
  1532.2 3.7 copy.139
  1535.9 3.7 copy.140
  1539.6 3.7 copy.141
  1544.7 16.2 reduce-scatter.17.cloned.1.call-done
  1560.9 5.1 multiply_subtract_fusion.2
  1566.1 24.0 %reduce-scatter.13.cloned.1.call-done = bf16[256,512]{1,0:T(8,128)(2,1)} async-done(((bf16[256,2048]{1,0:T(8,128)(2,1)}), bf16[256,512]{1,0:T(8,128)(2,1)}) %reduce-scatter.13.cloned.1.call-update) | async-done | bytes 262160 | tf_op jit(solution)/shard_map/reduce_scatter | solution.py:238
  1590.1 3.6 multiply_subtract_fusion.3
  1593.6 57.7 %reduce-scatter.11.cloned.1.call-done = bf16[512,3,256]{0,2,1:T(8,128)(2,1)} async-done(((bf16[2048,3,256]{0,2,1:T(8,128)(2,1)}), bf16[512,3,256]{0,2,1:T(8,128)(2,1)}) %reduce-scatter.11.cloned.1.call-update) | async-done | bytes 786448 | tf_op jit(solution)/shard_map/reduce_scatter | solution.py:235
  1651.3 5.5 multiply_subtract_fusion.1
  1666.4 59.7 %reduce-scatter.9.cloned.1.call-done = bf16[256,2048]{1,0:T(8,128)(2,1)} async-done(((bf16[2048,2048]{1,0:T(8,128)(2,1)}), bf16[256,2048]{1,0:T(8,128)(2,1)}) %reduce-scatter.9.cloned.1.call-update) | async-done | bytes 1048592 | tf_op jit(solution)/shard_map/reduce_scatter | solution.py:229
  1726.1 3.5 add_divide_fusion
  (201 shorter events, 96.3 us)
Async XLA Ops:
  7.2 3.3 copy-start.30
  7.2 6.0 copy-start.49
  7.2 6.0 copy-start.48
  7.2 69.1 %all-gather.10.cloned.1.call-start = ((), (), s32[]{:S(2)}) async-start(), calls=%async_computation.7 | async-start | bytes 3932160 | tf_op jit(solution)/shard_map/all_gather | solution.py:101
  9.7 121.5 %all-gather.8.cloned.1.call-start = ((), (), s32[]{:S(2)}) async-start(), calls=%async_computation.6 | async-start | bytes 9437184 | tf_op jit(solution)/shard_map/all_gather | solution.py:106
  10.5 175.8 %all-gather.12.cloned.1.call-start = ((), (), s32[]{:S(2)}) async-start(), calls=%async_computation.8 | async-start | bytes 1310720 | tf_op jit(solution)/shard_map/all_gather | solution.py:102
  11.3 992.9 %all-gather.14.cloned.1.call-start = ((), (), s32[]{:S(2)}) async-start(), calls=%async_computation.9 | async-start | bytes 7004160 | tf_op jit(solution)/shard_map/all_gather | solution.py:103
  13.2 150.0 %copy-start.28 = (f32[512,64]{1,0:T(8,128)}, f32[512,64]{1,0:T(8,128)S(1)}, u32[]{:S(2)}) copy-start(f32[512,64]{1,0:T(8,128)S(1)} %get-tuple-element.124) | copy-start | bytes 393220
  160.7 8.2 copy-start.15
  167.7 3.3 copy-start
  167.7 3.4 copy-start.36
  186.2 4.0 copy-start.2
  190.2 5.8 copy-start.1
  190.2 25.4 %collective-permute-start = (f32[2048,2048]{1,0:T(8,128)S(1)}, f32[2048,2048]{1,0:T(8,128)}, u32[]{:S(2)}, u32[]{:S(2)}) collective-permute-start(f32[2048,2048]{1,0:T(8,128)S(1)} %fusion.51), channel_id=1, source_target_pairs={{0,1},{1,0},{2,3},{3,2},{4,5},{5,4},{6,7},{7,6},{8,9},{9,8},{10,11... | collective-permute-start | bytes 50331656 | tf_op jit(solution)/shard_map/ppermute | solution.py:140
  227.2 375.8 %copy-start.4 = (f32[512,2,684]{0,1,2:T(2,128)S(1)}, f32[512,2,684]{0,1,2:T(2,128)}, u32[]{:S(2)}) copy-start(f32[512,2,684]{0,1,2:T(2,128)} %param.27) | copy-start | bytes 8404996
  227.2 362.6 %collective-permute-start.1 = (f32[2048,2048]{1,0:T(8,128)S(1)}, f32[2048,2048]{1,0:T(8,128)}, u32[]{:S(2)}, u32[]{:S(2)}) collective-permute-start(f32[2048,2048]{1,0:T(8,128)S(1)} %add.207), channel_id=1, source_target_pairs={{0,2},{1,3},{2,0},{3,1},{4,6},{5,7},{6,4},{7,5},{8,10},{9,11},{10,... | collective-permute-start | bytes 50331656 | tf_op jit(solution)/shard_map/ppermute | solution.py:140
  601.9 3.2 copy-start.20
  601.9 361.8 %collective-permute-start.2 = (f32[2048,2048]{1,0:T(8,128)}, f32[2048,2048]{1,0:T(8,128)}, u32[]{:S(2)}, u32[]{:S(2)}) collective-permute-start(f32[2048,2048]{1,0:T(8,128)} %add.208), channel_id=1, source_target_pairs={{0,4},{1,5},{2,6},{3,7},{4,0},{5,1},{6,2},{7,3},{8,12},{9,13},{10,... | collective-permute-start | bytes 50331656 | tf_op jit(solution)/shard_map/ppermute | solution.py:140
  605.1 426.9 %all-gather.16.cloned.1.call-start = ((), (), s32[]{:S(2)}) async-start(), calls=%async_computation.10 | async-start | bytes 3522560 | tf_op jit(solution)/shard_map/all_gather | solution.py:104
  606.1 564.0 %all-reduce.3.cloned.1.call-start = ((), (), s32[]{:S(2)}) async-start(), calls=%async_computation.11 | async-start | bytes 16777216 | tf_op jit(solution)/shard_map/psum | solution.py:152
  1031.9 11.8 copy-start.26
  1043.7 187.5 %all-gather.18.cloned.1.call-start = ((), (), s32[]{:S(2)}) async-start(), calls=%async_computation.12 | async-start | bytes 9437184 | tf_op jit(solution)/shard_map/all_gather | solution.py:159
  1044.4 128.3 %copy-start.22 = (bf16[256,2048]{1,0:T(8,128)(2,1)S(1)}, bf16[256,2048]{1,0:T(8,128)(2,1)}, u32[]{:S(2)}) copy-start(bf16[256,2048]{1,0:T(8,128)(2,1)} %param.21) | copy-start | bytes 3145732
  1176.7 162.1 %reduce-scatter.7.cloned.1.call-start = ((), (), s32[]{:S(2)}) async-start(), calls=%async_computation.13 | async-start | bytes 9437184 | tf_op jit(solution)/shard_map/reduce_scatter | solution.py:181
  1267.1 133.3 %all-gather.20.cloned.1.call-start = ((), (), s32[]{:S(2)}) async-start(), calls=%async_computation.14 | async-start | bytes 9437184 | tf_op jit(solution)/shard_map/all_gather | solution.py:188
  1345.9 181.0 %reduce-scatter.15.cloned.1.call-start = ((), (), s32[]{:S(2)}) async-start(), calls=%async_computation.18 | async-start | bytes 7045120 | tf_op jit(solution)/shard_map/reduce_scatter | solution.py:241
  1364.6 196.3 %reduce-scatter.17.cloned.1.call-start = ((), (), s32[]{:S(2)}) async-start(), calls=%async_computation.19 | async-start | bytes 3522560 | tf_op jit(solution)/shard_map/reduce_scatter | solution.py:244
  1377.1 23.3 %copy-start.32 = (bf16[256,2048]{1,0:T(8,128)(2,1)S(1)}, bf16[256,2048]{1,0:T(8,128)(2,1)}, u32[]{:S(2)}) copy-start(bf16[256,2048]{1,0:T(8,128)(2,1)} %all-gather.12.cloned.1.call-done) | copy-start | bytes 3145732
  1377.1 213.0 %reduce-scatter.13.cloned.1.call-start = ((), (), s32[]{:S(2)}) async-start(), calls=%async_computation.17 | async-start | bytes 1310720 | tf_op jit(solution)/shard_map/reduce_scatter | solution.py:238
  1413.2 3.8 copy-start.16
  1421.5 4.8 copy-start.11
  1421.5 4.8 copy-start.13
  1437.0 4.9 copy-start.3
  1441.9 6.9 copy-start.24
  1448.7 202.6 %reduce-scatter.11.cloned.1.call-start = ((), (), s32[]{:S(2)}) async-start(), calls=%async_computation.16 | async-start | bytes 3932160 | tf_op jit(solution)/shard_map/reduce_scatter | solution.py:235
  1462.9 263.2 %reduce-scatter.9.cloned.1.call-start = ((), (), s32[]{:S(2)}) async-start(), calls=%async_computation.15 | async-start | bytes 9437184 | tf_op jit(solution)/shard_map/reduce_scatter | solution.py:229
  1477.0 4.8 copy-start.47
  1477.0 5.4 copy-start.42
  1477.0 5.4 copy-start.43
  1478.6 48.3 %copy-start.5 = (f32[512,2,684]{0,1,2:T(2,128)S(1)}, f32[512,2,684]{0,1,2:T(2,128)}, u32[]{:S(2)}) copy-start(f32[512,2,684]{0,1,2:T(2,128)} %param.27) | copy-start | bytes 8404996
  1539.6 3.7 copy-start.39
  1539.6 3.7 copy-start.44
  1539.6 3.7 copy-start.45
  1539.6 21.3 %copy-start.21 = (f32[684,512]{1,0:T(8,128)S(1)}, f32[684,512]{1,0:T(8,128)}, u32[]{:S(2)}) copy-start(f32[684,512]{1,0:T(8,128)} %param.28) | copy-start | bytes 4202500
  1539.6 21.3 %copy-start.31 = (f32[684,512]{1,0:T(8,128)S(1)}, f32[684,512]{1,0:T(8,128)}, u32[]{:S(2)}) copy-start(f32[684,512]{1,0:T(8,128)} %param.33) | copy-start | bytes 4202500
  1566.1 85.2 %copy-start.18 = (f32[512,3,256]{0,2,1:T(8,128)S(1)}, f32[512,3,256]{0,2,1:T(8,128)}, u32[]{:S(2)}) copy-start(f32[512,3,256]{0,2,1:T(8,128)} %copy.131) | copy-start | bytes 4718596
  1566.1 85.2 %copy-start.19 = (f32[512,3,256]{0,2,1:T(8,128)S(1)}, f32[512,3,256]{0,2,1:T(8,128)}, u32[]{:S(2)}) copy-start(f32[512,3,256]{0,2,1:T(8,128)} %copy.127) | copy-start | bytes 4718596
  1659.8 66.2 %copy-start.14 = (f32[256,2048]{1,0:T(8,128)S(1)}, f32[256,2048]{1,0:T(8,128)}, u32[]{:S(2)}) copy-start(f32[256,2048]{1,0:T(8,128)} %get-tuple-element.94) | copy-start | bytes 6291460
  (21 other events, 38.5 us)
Sparse Core Ops, SparseCore 0:
  10.2 66.1 all-gather.9
  78.3 52.8 all-gather.7
  133.3 27.9 all-gather.11
  605.2 103.9 all-gather.13
  711.1 56.2 all-gather.15
  1043.8 126.1 all-reduce.2
  1176.8 54.3 all-gather.17
  1267.2 71.4 reduce-scatter.6
  1346.0 54.2 all-gather.19
  1402.5 100.1 reduce-scatter.14
  1505.0 55.8 reduce-scatter.16
  1563.1 26.9 reduce-scatter.12
  1592.4 58.9 reduce-scatter.10
  1654.6 71.3 reduce-scatter.8
